TPU v7x, 512 devices: a whole 4x4x16 slice. The times are simulated.
512 devices in a mesh: row: 16 (over y_hi, x, core), col: 32 (over z, y_lo).
Axes of the slice: x: 4, y: 4 (y_hi: 2, y_lo: 2; y = y_hi * 2 + y_lo), z: 16, core: 2. Of those that a mesh axis runs over, the one named last changes fastest.
Arguments:
- history: bfloat16 [16, 32, 32, 8, 128], P('row', 'col'), may hold values from -6 to 6
- tiles: bfloat16 [16, 32, 96, 128, 128], P('row', 'col'), may hold values from -0.078125 to 0.078125
- tile_target: int32 [16, 32, 96], P('row', 'col'), may hold values from 0 to 31
- tile_lag: int32 [16, 32, 96], P('row', 'col'), may hold values from 16 to 32
- tile_count: int32 [16, 32, 16], P('row', 'col'), may hold values from 0 to 6, as said below
- self_tiles: bfloat16 [16, 32, 32, 128, 128], P('row', 'col'), may hold values from -0.046875 to 0.046875
- near_inverse: float32 [16, 32, 128, 128], P('row', 'col'), may hold values from -0.5 to 0.5
- incident: float32 [16, 32, 16, 8, 128], P('row', 'col'), may hold values from -6 to 6
Outputs:
- density: float32 [16, 32, 16, 8, 128], P('row', 'col')
Inputs may be any that keep to these rules, and one draw needn't show every extreme that they name: tile_count[g, c, h] is the number of live slots h * 6 .. h * 6 + 5 of device (g, c), which come first in that range; the other slots' entries are not read. Every device has 6 live slots for at least one row h.
All inputs are finite; a program needn't handle non-finite values.
Results may differ from a plain program's by a relative error of at most 0.0007.
Values may be sent and summed in bfloat16 or wider, within the bound.
No kernel may reach another device: no remote copies, remote signals or barrier semaphores. Data moves between devices by JAX's collectives and lax.ppermute only.
A program may use at most 64 MiB of HBM per device.

v0:
```python
import jax
import jax.numpy as jnp
from jax import lax
from jax.sharding import PartitionSpec as P


def local(history, tiles, tile_target, tile_lag, tile_count, self_tiles, near_inverse, incident):
    groups = lax.axis_size("row")
    panels = lax.axis_size("col")
    hist_steps = history.shape[2]
    excite = history.shape[3]
    block = history.shape[4]
    steps = incident.shape[2]
    own_tiles = tiles[0, 0]
    slots_dev = own_tiles.shape[0]
    per_source = slots_dev // groups
    targets_all = tile_target[0, 0]
    lags_all = tile_lag[0, 0]
    counts_all = tile_count[0, 0]
    step_range = jnp.arange(steps, dtype=jnp.int32)
    panel_range = jnp.arange(panels, dtype=jnp.int32)
    empty = jnp.zeros((panels, steps, excite, block), jnp.float32)
    source_piece = lax.all_gather(history, "row", axis=0, tiled=True)
    rows_here = source_piece.shape[0]
    width = rows_here * per_source
    flat_past = source_piece.reshape(rows_here * hist_steps, excite, block)
    slot_range = jnp.arange(width, dtype=jnp.int32)
    local_group = slot_range // per_source
    within_group = slot_range % per_source
    group_match = local_group[:, None] == jnp.arange(rows_here, dtype=jnp.int32)[None, :]
    live = jnp.any(group_match & (within_group[:, None] < counts_all[None, :]), axis=1)
    rows_index = (
        local_group[:, None] * hist_steps + hist_steps - lags_all[:, None] + step_range[None, :]
    )
    windows = jnp.take(flat_past, rows_index, axis=0)
    products = jnp.einsum("skej,sji->skei", windows, own_tiles, preferred_element_type=jnp.float32)
    selector = ((targets_all[None, :] == panel_range[:, None]) & live[None, :]).astype(jnp.float32)
    selector, flat_products = (selector, products.reshape(width, steps * excite * block))
    summed = jnp.dot(
        selector, flat_products, precision=lax.Precision.HIGHEST, preferred_element_type=jnp.float32
    )
    partial_value = summed.reshape(empty.shape)
    far = lax.psum_scatter(partial_value, "col", scatter_dimension=0, tiled=True)[0]
    own_past = history[0, 0]
    own_self = self_tiles[0, 0]
    lag_range = jnp.arange(hist_steps, dtype=jnp.int32) + 1
    before = lag_range[:, None] > step_range[None, :]
    past_index = jnp.where(before, hist_steps + step_range[None, :] - lag_range[:, None], 0)
    self_windows = jnp.take(own_past, past_index, axis=0) * before[:, :, None, None].astype(
        jnp.bfloat16
    )
    self_past = jnp.einsum(
        "lkej,lji->kei", self_windows, own_self, preferred_element_type=jnp.float32
    )
    near_matrix = near_inverse[0, 0]
    drive = incident[0, 0] - far - self_past
    fresh_list = []
    density_list = []
    for step_index in range(steps):
        bracket = drive[step_index]
        if step_index > 0:
            earlier = jnp.stack(fresh_list, axis=0)
            lagged = own_self[:step_index][::-1]
            bracket = bracket - jnp.einsum(
                "lej,lji->ei", earlier, lagged, preferred_element_type=jnp.float32
            )
        density_now = jnp.dot(
            bracket,
            near_matrix,
            precision=lax.Precision.HIGHEST,
            preferred_element_type=jnp.float32,
        )
        density_list.append(density_now)
        fresh_list.append(density_now.astype(jnp.bfloat16))
    return jnp.stack(density_list, axis=0)[None, None]


def solution(mesh):
    return jax.shard_map(
        local,
        mesh=mesh,
        in_specs=(
            P("row", "col", None, None, None),
            P("row", "col", None, None, None),
            P("row", "col", None),
            P("row", "col", None),
            P("row", "col", None),
            P("row", "col", None, None, None),
            P("row", "col", None, None),
            P("row", "col", None, None, None),
        ),
        out_specs=P("row", "col", None, None, None),
        check_vma=False,
    )
```

profile of v0, /device:TPU:4, one launch (start us, length us, event | category | flops | bytes accessed | tf_op | source)
XLA Modules:
  0.0 256.7 jit_solution(12869515041279150082)
XLA Ops:
  6.5 0.7 all-gather.2.cloned.1.call-update
  7.3 0.8 bitcast_subtract_fusion.1
  8.5 0.7 fusion.109
  9.2 64.6 %all-gather.2.cloned.1.call-done = bf16[16,1,32,8,128]{4,3,2,1,0:T(8,128)(2,1)} async-done(((bf16[1,1,32,8,128]{4,3,2,1,0:T(8,128)(2,1)}), bf16[16,1,32,8,128]{4,3,2,1,0:T(8,128)(2,1)}) %all-gather.2.cloned.1.call-update) | async-done | bytes 1048592 | tf_op jit(solution)/shard_map/all_gather | solution.py:23
  73.9 5.0 %gather_fusion = bf16[1536,8,128]{2,1,0:T(8,128)(2,1)} fusion(bf16[512,8,128]{2,1,0:T(8,128)(2,1)} %bitcast.437, s32[2048]{0:T(1024)S(1)} %pad_clamp_fusion), kind=kCustom, calls=%fused_computation | custom fusion | bytes 6297600 | tf_op jit(solution)/shard_map/jit(_take)/gather | solution.py:35
  78.9 6.3 %fusion.2 = f32[96,16,8,128]{3,2,1,0:T(8,128)S(1)} fusion(bf16[1,1,96,128,128]{4,3,2,1,0:T(8,128)(2,1)S(1)} %copy-done, bf16[96,16,8,128]{3,2,1,0:T(8,128)(2,1)} %bitcast.434, pred[96,16]{1,0:T(8,128)(4,1)S(1)} %copy.18), kind=kOutput, calls=%fused_computation.5 | convolution fusion | flops 404226048 | bytes 12584448 | tf_op jit(solution)/shard_map/skej,sji->skei/dot_general | solution.py:36
  85.2 4.4 %copy.34 = f32[12,8,128,128]{3,1,2,0:T(8,128)S(1)} copy(f32[12,8,128,128]{3,2,1,0:T(8,128)S(1)} %bitcast.433) | data formatting | bytes 12582912
  89.6 1.1 copy.26
  90.7 5.9 %fusion = f32[32,16,8,128]{3,0,2,1:T(8,128)S(1)} fusion(f32[16,8,128,96]{2,1,0,3:T(8,128)S(1)} %bitcast.435, s32[96]{0:T(128)S(1)} %bitcast.439, pred[96]{0:T(512)(128)(4,1)S(1)} %fusion.109), kind=kOutput, calls=%fused_computation.3 | convolution fusion | flops 603985920 | bytes 8389088 | tf_op jit(solution)/shard_map/dot_general | solution.py:39
  96.6 2.8 %copy.20 = f32[32,16,8,128]{3,2,1,0:T(8,128)} copy(f32[32,16,8,128]{3,0,2,1:T(8,128)S(1)} %fusion) | data formatting | bytes 4194304 | tf_op jit(solution)/shard_map/dot_general | solution.py:39
  99.6 2.4 gather_fusion.1
  102.0 138.8 %reduce-scatter.2.cloned.1.call-done = f32[1,16,8,128]{3,2,1,0:T(8,128)} async-done(((f32[32,16,8,128]{3,2,1,0:T(8,128)}), f32[1,16,8,128]{3,2,1,0:T(8,128)}) %reduce-scatter.2.cloned.1.call-update) | async-done | bytes 65552 | tf_op jit(solution)/shard_map/reduce_scatter | solution.py:43
  240.8 2.9 %fusion.7 = f32[16,8,128]{2,1,0:T(8,128)S(1)} fusion(bf16[1,1,32,128,128]{4,3,2,1,0:T(8,128)(2,1)} %param.13, bf16[32,16,8,128]{3,2,1,0:T(8,128)(2,1)} %bitcast.438, pred[32,16]{0,1:T(8,128)(4,1)S(1)} %get-tuple-element.127, bf16[32,16]{0,1:T(8,128)(2,1)S(1)} %get-tuple-element.126, f32[1,16,8,128]{3,2,1,0:T(8,128)} %reduce-scatter.2.cloned.1.call-done, ...), kind=kOutput, calls=%fused_computation.11 | convolution fusion | flops 135299072 | bytes 2295296 | tf_op jit(solution)/shard_map/lkej,lji->kei/dot_general | solution.py:52
  244.1 0.2 constant_dynamic-update-slice_fusion.123
  244.4 0.2 constant_dynamic-update-slice_fusion.122
  244.7 0.2 constant_dynamic-update-slice_fusion.121
  245.5 0.2 constant_dynamic-update-slice_fusion.119
  245.8 0.2 constant_dynamic-update-slice_fusion.118
  246.7 0.2 fusion.12
  246.9 0.2 constant_dynamic-update-slice_fusion.115
  247.1 0.2 fusion.11
  247.2 0.2 constant_dynamic-update-slice_fusion.114
  247.4 0.2 fusion.8
  247.6 0.2 constant_dynamic-update-slice_fusion.113
  247.8 0.2 fusion.22
  248.1 0.2 fusion.9
  248.3 0.2 constant_dynamic-update-slice_fusion.111
  248.5 0.2 fusion.21
  248.7 0.2 constant_dynamic-update-slice_fusion.110
  248.9 0.2 fusion.10
  249.1 0.2 fusion.20
  249.2 0.7 copy-done.5
  (68 shorter events, 3.0 us)
Async XLA Ops:
  6.5 72.4 %copy-start = (bf16[1,1,96,128,128]{4,3,2,1,0:T(8,128)(2,1)S(1)}, bf16[1,1,96,128,128]{4,3,2,1,0:T(8,128)(2,1)}, u32[]{:S(2)}) copy-start(bf16[1,1,96,128,128]{4,3,2,1,0:T(8,128)(2,1)} %param.9) | copy-start | bytes 9437188
  6.5 67.3 %all-gather.2.cloned.1.call-start = ((), (), s32[]{:S(2)}) async-start(), calls=%async_computation.1 | async-start | bytes 1114112 | tf_op jit(solution)/shard_map/all_gather | solution.py:23
  7.3 233.5 %reduce-scatter.2.cloned.1.call-start = ((), (), s32[]{:S(2)}) async-start(), calls=%async_computation.2 | async-start | bytes 2162688 | tf_op jit(solution)/shard_map/reduce_scatter | solution.py:43
  89.5 1.1 copy-start.4
  96.6 3.0 %copy-start.1 = (bf16[1,1,32,8,128]{4,3,2,1,0:T(8,128)(2,1)S(1)}, bf16[1,1,32,8,128]{4,3,2,1,0:T(8,128)(2,1)}, u32[]{:S(2)}) copy-start(bf16[1,1,32,8,128]{4,3,2,1,0:T(8,128)(2,1)} %param.8) | copy-start | bytes 196612
  99.4 141.4 %copy-start.6 = (f32[1,1,16,8,128]{4,3,2,1,0:T(8,128)S(1)}, f32[1,1,16,8,128]{4,3,2,1,0:T(8,128)}, u32[]{:S(2)}) copy-start(f32[1,1,16,8,128]{4,3,2,1,0:T(8,128)} %param.15) | copy-start | bytes 196612
  102.0 141.8 %copy-start.2 = (f32[1,1,128,128]{3,2,1,0:T(8,128)S(1)}, f32[1,1,128,128]{3,2,1,0:T(8,128)}, u32[]{:S(2)}) copy-start(f32[1,1,128,128]{3,2,1,0:T(8,128)} %param.14) | copy-start | bytes 196612
  240.8 3.1 %copy-start.3 = (bf16[1,1,32,128,128]{4,3,2,1,0:T(8,128)(2,1)S(1)}, bf16[1,1,32,128,128]{4,3,2,1,0:T(8,128)(2,1)}, u32[]{:S(2)}) copy-start(bf16[1,1,32,128,128]{4,3,2,1,0:T(8,128)(2,1)} %param.13) | copy-start | bytes 3145732
  249.2 0.7 copy-start.5
Sparse Core Ops, SparseCore 0:
  10.6 63.1 all-gather.1
  99.5 141.2 reduce-scatter.1
where the time goes:
time: 257 us
  waiting for transfers between devices  204 us (79%)
  matrix products  20.1 us (8%)
  local copies, waits for them, and re-layouts  16.9 us (7%)
  between operations  13.6 us (5%)
    reduce_scatter x1, waiting for transfers between devices, local(): lax.psum_scatter(partial_value, 'col', scatter_dimension=0, tiled=True)[0]  139 us
    all_gather x1, waiting for transfers between devices, local(): source_piece = lax.all_gather(history, 'row', axis=0, tiled=True)  64.6 us
    unnamed x42, local copies, waits for them, and re-layouts  6.47 us
    dot_general x1, matrix products, local(): jnp.einsum('skej,sji->skei', windows, own_tiles, preferred_element_type=j...  6.28 us
    dot_general x1, matrix products, local(): jnp.dot(selector, flat_products, precision=lax.Precision.HIGHEST, preferr...  5.92 us
  transfers between devices with their start and end apart: 2, of which 2 were waited for; matrix products, arithmetic and copies ran while one was open for 2% of the time, Pallas kernels for 0%

commit v1 on v0

v1 whole, which is shorter than its diff:
```python
import functools

import jax
import jax.numpy as jnp
from jax import lax
from jax.experimental import pallas as pl
from jax.experimental.pallas import tpu as pltpu
from jax.sharding import Mesh, PartitionSpec as P

B = 128
E = 8
HIST = 32
K = 16
TPS = 6
GROUPS = 16
PANELS = 32
SLOTS = 96
ROWS = K * E
HALF = GROUPS // 2
CODE = 8
FULL = 32760.0

VMEM = pl.BlockSpec(memory_space=pltpu.VMEM)
SMEM = pl.BlockSpec(memory_space=pltpu.SMEM)
HIGHEST = lax.Precision.HIGHEST


def dot(a, b):
    return jnp.dot(a, b, preferred_element_type=jnp.float32)


def encode(values, store):
    peak = jnp.maximum(jnp.max(jnp.abs(values), axis=0, keepdims=True), 1e-30)
    code = jnp.floor(jnp.log2(peak)) + 1.0
    scaled = values * (jnp.exp2(-code) * FULL)
    store(0, ROWS, jnp.round(scaled).astype(jnp.int32).astype(jnp.int16))
    wide = jnp.broadcast_to(code, (CODE, B))
    store(ROWS, CODE, wide.astype(jnp.int32).astype(jnp.int16))


def decode(block):
    code = block[ROWS : ROWS + 1].astype(jnp.int32).astype(jnp.float32)
    scale = jnp.exp2(code) * (1.0 / FULL)
    return block[:ROWS].astype(jnp.int32).astype(jnp.float32) * scale


def add_products(side, lag, target, count, past, tiles, wide, total):
    wide[...] = past[...].astype(jnp.float32)

    def source(p, carry):
        h = 2 * p + side
        live = count[h]
        for j in range(TPS):
            s = h * TPS + j
            first = jnp.clip(HIST - lag[s], 0, HIST - K)
            place = jnp.where(j < live, jnp.clip(target[s], 0, PANELS - 1), PANELS)
            window = wide[p, pl.ds(first, K)].reshape(ROWS, B).astype(jnp.bfloat16)
            total[place] += dot(window, tiles[s])
        return carry

    lax.fori_loop(0, HALF, source, 0)


def near_kernel(core, lag, target, count, past, tiles, total, wide):
    total[...] = jnp.zeros_like(total)
    add_products(core[0], lag, target, count, past, tiles, wide, total)


def far_kernel(core, lag, target, count, past, tiles, before, out, wide, total):
    total[...] = before[...]
    add_products(1 - core[0], lag, target, count, past, tiles, wide, total)

    def pack(z, carry):
        for d in range(4):

            def store(at, n, v):
                out[d, z, pl.ds(at, n)] = v

            encode(total[z * 4 + d], store)
        return carry

    lax.fori_loop(0, PANELS // 4, pack, 0)


def merge_kernel(got, out):
    def merge(z, carry):
        value = decode(got[0, z])
        for d in range(1, 4):
            value = value + decode(got[d, z])

        def store(at, n, v):
            out[z, pl.ds(at, n)] = v

        encode(value, store)
        return carry

    lax.fori_loop(0, PANELS // 4, merge, 0)


def thirds(x):
    a = x.astype(jnp.bfloat16)
    rest = x - a.astype(jnp.float32)
    b = rest.astype(jnp.bfloat16)
    c = (rest - b.astype(jnp.float32)).astype(jnp.bfloat16)
    return a, b, c


def self_kernel(own, self_tiles, near, incident, base, steps, wide):
    wide[pl.ds(0, HIST)] = own[...].astype(jnp.float32)
    wide[pl.ds(HIST, K)] = jnp.zeros((K, E, B), jnp.float32)
    drive = incident[...].reshape(ROWS, B)
    for lag in range(1, HIST + 1):
        window = wide[pl.ds(HIST - lag, K)].reshape(ROWS, B).astype(jnp.bfloat16)
        drive = drive - dot(window, self_tiles[lag - 1])
    base[...] = jnp.dot(drive, near[...], precision=HIGHEST, preferred_element_type=jnp.float32)
    a, b, c = thirds(near[...])
    for lag in range(1, K):
        tile = self_tiles[lag - 1]
        m = dot(tile, a) + dot(tile, b) + dot(tile, c)
        high = m.astype(jnp.bfloat16)
        steps[lag - 1, pl.ds(0, B)] = high
        steps[lag - 1, pl.ds(B, B)] = (m - high.astype(jnp.float32)).astype(jnp.bfloat16)


def solve_kernel(got, near, base, steps, density):
    far = decode(got[0])
    for z in range(1, PANELS // 4):
        far = far + decode(got[z])
    drive = base[...] - jnp.dot(far, near[...], precision=HIGHEST, preferred_element_type=jnp.float32)
    rest = [drive[E * k : E * (k + 1)] for k in range(K)]
    for k in range(K):
        density[k] = rest[k]
        fresh = rest[k].astype(jnp.bfloat16)
        twice = jnp.concatenate([fresh, fresh], axis=1)
        for j in range(k + 1, K):
            rest[j] = rest[j] - dot(twice, steps[j - k - 1])


def call(kernel, outs, n_scalar, n_vector, scratch=(), **kw):
    single = not isinstance(outs, (tuple, list))
    return pl.pallas_call(
        kernel,
        out_shape=outs,
        in_specs=[SMEM] * n_scalar + [VMEM] * n_vector,
        out_specs=VMEM if single else [VMEM] * len(outs),
        scratch_shapes=list(scratch),
        compiler_params=pltpu.CompilerParams(vmem_limit_bytes=kw.get("limit", 24) << 20),
        cost_estimate=pl.CostEstimate(flops=kw.get("flops", 4 << 20), bytes_accessed=kw.get("bytes", 1 << 20), transcendentals=0),
        name=kw["name"],
    )


def local(history, tiles, tile_target, tile_lag, tile_count, self_tiles, near_inverse, incident):
    own = history[0, 0]
    core = lax.axis_index("core").astype(jnp.int32)[None]
    lag, target, count = tile_lag[0, 0], tile_target[0, 0], tile_count[0, 0]
    slot_tiles, near = tiles[0, 0], near_inverse[0, 0]
    wide = pltpu.VMEM((HALF, HIST, E, B), jnp.float32)
    total = jax.ShapeDtypeStruct((PANELS + 1, ROWS, B), jnp.float32)

    same = lax.all_to_all(jnp.broadcast_to(own, (HALF, HIST, E, B)), ("y_hi", "x"), 0, 0, tiled=True)
    other = lax.ppermute(same, "core", [(0, 1), (1, 0)])
    partial = call(near_kernel, total, 4, 2, [wide], name="near", flops=48 << 22, bytes=4 << 20)(
        core, lag, target, count, same, slot_tiles
    )
    base, steps = call(
        self_kernel,
        [jax.ShapeDtypeStruct((ROWS, B), jnp.float32), jax.ShapeDtypeStruct((K - 1, 2 * B, B), jnp.bfloat16)],
        0,
        4,
        [pltpu.VMEM((HIST + K, E, B), jnp.float32)],
        name="selfpast",
        flops=32 << 22,
        bytes=2 << 20,
    )(own, self_tiles[0, 0], near, incident[0, 0])
    blocks = call(
        far_kernel,
        jax.ShapeDtypeStruct((4, PANELS // 4, ROWS + CODE, B), jnp.int16),
        4,
        3,
        [wide, pltpu.VMEM((PANELS + 1, ROWS, B), jnp.float32)],
        name="far",
        flops=48 << 22,
        bytes=6 << 20,
    )(core, lag, target, count, other, slot_tiles, partial)
    got = lax.all_to_all(blocks, ("z_lo", "y_lo"), 0, 0, tiled=True)
    merged = call(
        merge_kernel, jax.ShapeDtypeStruct((PANELS // 4, ROWS + CODE, B), jnp.int16), 0, 1, name="merge"
    )(got)
    got = lax.all_to_all(merged, "z_hi", 0, 0, tiled=True)
    density = call(solve_kernel, jax.ShapeDtypeStruct((K, E, B), jnp.float32), 0, 4, name="solve")(
        got, near, base, steps
    )
    return density[None, None]


def solution(mesh):
    fine = Mesh(mesh.devices.reshape(2, 4, 2, 8, 2, 2), ("y_hi", "x", "core", "z_hi", "z_lo", "y_lo"))
    row, col = ("y_hi", "x", "core"), ("z_hi", "z_lo", "y_lo")
    return jax.shard_map(
        local,
        mesh=fine,
        in_specs=(
            P(row, col, None, None, None),
            P(row, col, None, None, None),
            P(row, col, None),
            P(row, col, None),
            P(row, col, None),
            P(row, col, None, None, None),
            P(row, col, None, None),
            P(row, col, None, None, None),
        ),
        out_specs=P(row, col, None, None, None),
        check_vma=False,
    )
```

time: 257 us -> 89.3 us (0.35)
  the two profiles are of different devices: /device:TPU:4 before, /device:TPU:8 now
where the time goes in v1:
time: 89.3 us; the launch traced here: 88.9 us
  blocking collectives  36.4 us (41%)
  waiting for transfers between devices  20.5 us (23%)
  starting transfers between devices  16.6 us (19%)
  Pallas kernels  10.5 us (12%)
  local copies, waits for them, and re-layouts  4.78 us (5%)
    all_to_all x1, waiting for transfers between devices, local(): got = lax.all_to_all(merged, 'z_hi', 0, 0, tiled=True)  20.5 us
    all_to_all x1, blocking collectives, local(): got = lax.all_to_all(blocks, ('z_lo', 'y_lo'), 0, 0, tiled=True)  19 us
    all_to_all x1, blocking collectives, local(): lax.all_to_all(jnp.broadcast_to(own, (HALF, HIST, E, B)), ('y_hi', 'x'),...  17.4 us
    all_to_all x1, starting transfers between devices, local(): got = lax.all_to_all(merged, 'z_hi', 0, 0, tiled=True)  14.7 us
    unnamed x18, local copies, waits for them, and re-layouts  3.88 us
    pallas_call x1, Pallas kernels, local(): call(far_kernel, jax.ShapeDtypeStruct((4, PANELS // 4, ROWS + CODE, B), j...  3 us
    pallas_call x1, Pallas kernels, local(): call(solve_kernel, jax.ShapeDtypeStruct((K, E, B), jnp.float32), 0, 4, na...  2.73 us
    pallas_call x1, Pallas kernels, local(): call(near_kernel, total, 4, 2, [wide], name='near', flops=48 << 22, bytes...  2.47 us
  transfers between devices with their start and end apart: 2, of which 1 were waited for; matrix products, arithmetic and copies ran while one was open for 0% of the time, Pallas kernels for 4%

profile of v1, /device:TPU:8, one launch (start us, length us, event | category | flops | bytes accessed | tf_op | source)
XLA Modules:
  0.0 88.9 jit_solution(2228082050348946251)
XLA Ops:
  0.0 0.9 %broadcast_in_dim.10 = bf16[8,32,8,128]{3,2,1,0:T(8,128)(2,1)S(1)} broadcast(bf16[32,8,128]{2,1,0:T(8,128)(2,1)} %bitcast.13), dimensions={1,2,3} | broadcast | bytes 589824 | tf_op jit(solution)/shard_map/broadcast_in_dim | solution.py:161
  0.9 17.4 %all_to_all.15.past = bf16[8,32,8,128]{3,2,1,0:T(8,128)(2,1)S(1)} all-to-all(bf16[8,32,8,128]{3,2,1,0:T(8,128)(2,1)S(1)} %broadcast_in_dim.10), channel_id=1, replica_groups=mesh['y_hi'=2,'x'=4,'core'=2,'z_hi'=8,'z_lo'=2,'y_lo'=2] {'y_hi','x'}, dimensions={0} | all-to-all | bytes 1048576 | tf_op jit(solution)/shard_map/all_to_all | solution.py:161
  18.3 1.9 %collective-permute-start = (bf16[8,32,8,128]{3,2,1,0:T(8,128)(2,1)S(1)}, bf16[8,32,8,128]{3,2,1,0:T(8,128)(2,1)S(1)}, u32[]{:S(2)}, u32[]{:S(2)}) collective-permute-start(bf16[8,32,8,128]{3,2,1,0:T(8,128)(2,1)S(1)} %all_to_all.15.past), channel_id=1, source_target_pairs={{0,32},{32,0},{1,33},{33,1},{2,34},{34,2},{3,35},{35,3},{4,36},{36... | collective-permute-start | bytes 1572872 | tf_op jit(solution)/shard_map/ppermute | solution.py:162
  20.2 0.0 copy-start
  20.3 1.9 %copy-done = bf16[1,1,96,128,128]{4,3,2,1,0:T(8,128)(2,1)S(1)} copy-done((bf16[1,1,96,128,128]{4,3,2,1,0:T(8,128)(2,1)S(1)}, bf16[1,1,96,128,128]{4,3,2,1,0:T(8,128)(2,1)}, u32[]{:S(2)}) %copy-start) | copy-done | bytes 3145752
  22.1 0.0 copy-start.6
  22.1 0.7 copy-done.6
  22.8 0.0 copy-start.7
  22.8 0.7 copy-done.7
  23.5 0.0 copy-start.8
  23.5 0.7 copy-done.8
  24.1 0.0 copy-start.1
  24.1 2.5 %near.1.before = f32[33,128,128]{2,1,0:T(8,128)S(1)} custom-call(s32[1]{0:T(128)} %bitcast.core, s32[96]{0:T(128)S(1)} %bitcast.18, s32[96]{0:T(128)S(1)} %bitcast.20, s32[16]{0:T(128)S(1)} %bitcast.22, bf16[8,32,8,128]{3,2,1,0:T(8,128)(2,1)S(1)} %all_to_all.15.past, bf16[96,128,128]{2,1,0:T(8,128)(2,1)S(1)} %bitcast.10), custom_call_target="tpu_custom_call" | custom-call | flops 201326592 | bytes 4194304 | tf_op jit(solution)/shard_map/near/pallas_call | solution.py:163
  26.6 0.0 collective-permute-done.past
  26.6 0.0 copy-done.1
  26.6 3.0 %far.1 = s16[4,8,136,128]{3,2,1,0:T(8,128)(2,1)S(1)} custom-call(s32[1]{0:T(128)} %bitcast.core, s32[96]{0:T(128)S(1)} %bitcast.19, s32[96]{0:T(128)S(1)} %bitcast.21, s32[16]{0:T(128)S(1)} %bitcast.23, bf16[8,32,8,128]{3,2,1,0:T(8,128)(2,1)S(1)} %collective-permute-done.past, bf16[96,128,128]{2,1,0:T(8,128)(2,1)S(1)} %bitcast.11, ...), custom_call_target="tpu_custom_call" | custom-call | flops 201326592 | bytes 6291456 | tf_op jit(solution)/shard_map/far/pallas_call | solution.py:176
  29.6 0.0 copy-start.2
  29.6 0.0 copy-start.3
  29.6 0.0 copy-start.4
  29.6 0.0 copy-start.5
  29.7 19.0 %all_to_all.16.got = s16[4,8,136,128]{3,2,1,0:T(8,128)(2,1)S(1)} all-to-all(s16[4,8,136,128]{3,2,1,0:T(8,128)(2,1)S(1)} %far.1), channel_id=1, replica_groups=mesh['y_hi'=2,'x'=4,'core'=2,'z_hi'=8,'z_lo'=2,'y_lo'=2] {'z_lo','y_lo'}, dimensions={0} | all-to-all | bytes 2228224 | tf_op jit(solution)/shard_map/all_to_all | solution.py:186
  48.6 1.3 %merge.1 = s16[8,136,128]{2,1,0:T(8,128)(2,1)} custom-call(s16[4,8,136,128]{3,2,1,0:T(8,128)(2,1)S(1)} %all_to_all.16.got), custom_call_target="tpu_custom_call" | custom-call | flops 4194304 | bytes 1048576 | tf_op jit(solution)/shard_map/merge/pallas_call | solution.py:187
  49.9 14.7 %all-to-all-start.2 = ((s16[8,136,128]{2,1,0:T(8,128)(2,1)}), s16[8,136,128]{2,1,0:T(8,128)(2,1)S(1)}, u32[]{:S(2)}, u32[]{:S(2)}) async-start(s16[8,136,128]{2,1,0:T(8,128)(2,1)} %merge.1), calls=%async_computation.2 | async-start | bytes 557056 | tf_op jit(solution)/shard_map/all_to_all | solution.py:190
  64.6 0.0 copy-done.2
  64.6 0.0 copy-done.3
  64.6 0.0 copy-done.4
  64.6 0.0 copy-done.5
  64.6 1.0 %selfpast.1 = (f32[128,128]{1,0:T(8,128)S(1)}, bf16[15,256,128]{2,1,0:T(8,128)(2,1)S(1)}) custom-call(bf16[32,8,128]{2,1,0:T(8,128)(2,1)S(1)} %bitcast.14, bf16[32,128,128]{2,1,0:T(8,128)(2,1)S(1)} %bitcast.12, f32[128,128]{1,0:T(8,128)S(1)} %bitcast.15, f32[16,8,128]{2,1,0:T(8,128)S(1)} %bitcast.17), custom_call_target="tpu_custom_call" | custom-call | flops 134217728 | bytes 2097152 | tf_op jit(solution)/shard_map/selfpast/pallas_call | solution.py:166
  65.6 20.5 %all-to-all-done.2.got = s16[8,136,128]{2,1,0:T(8,128)(2,1)S(1)} async-done(((s16[8,136,128]{2,1,0:T(8,128)(2,1)}), s16[8,136,128]{2,1,0:T(8,128)(2,1)S(1)}, u32[]{:S(2)}, u32[]{:S(2)}) %all-to-all-start.2) | async-done | bytes 278560 | tf_op jit(solution)/shard_map/all_to_all | solution.py:190
  86.2 2.7 %solve.1 = f32[16,8,128]{2,1,0:T(8,128)} custom-call(s16[8,136,128]{2,1,0:T(8,128)(2,1)S(1)} %all-to-all-done.2.got, f32[128,128]{1,0:T(8,128)S(1)} %bitcast.16, f32[128,128]{1,0:T(8,128)S(1)} %get-tuple-element.7.base, bf16[15,256,128]{2,1,0:T(8,128)(2,1)S(1)} %get-tuple-element.8.steps), custom_call_target="tpu_custom_call" | custom-call | flops 4194304 | bytes 1048576 | tf_op jit(solution)/shard_map/solve/pallas_call | solution.py:191
Async XLA Ops:
  18.3 8.3 %collective-permute-start = (bf16[8,32,8,128]{3,2,1,0:T(8,128)(2,1)S(1)}, bf16[8,32,8,128]{3,2,1,0:T(8,128)(2,1)S(1)}, u32[]{:S(2)}, u32[]{:S(2)}) collective-permute-start(bf16[8,32,8,128]{3,2,1,0:T(8,128)(2,1)S(1)} %all_to_all.15.past), channel_id=1, source_target_pairs={{0,32},{32,0},{1,33},{33,1},{2,34},{34,2},{3,35},{35,3},{4,36},{36... | collective-permute-start | bytes 1572872 | tf_op jit(solution)/shard_map/ppermute | solution.py:162
  20.2 1.9 %copy-start = (bf16[1,1,96,128,128]{4,3,2,1,0:T(8,128)(2,1)S(1)}, bf16[1,1,96,128,128]{4,3,2,1,0:T(8,128)(2,1)}, u32[]{:S(2)}) copy-start(bf16[1,1,96,128,128]{4,3,2,1,0:T(8,128)(2,1)} %param.9) | copy-start | bytes 9437188
  22.1 0.7 copy-start.6
  22.8 0.7 copy-start.7
  23.5 0.7 copy-start.8
  24.1 2.5 %copy-start.1 = (bf16[1,1,96,128,128]{4,3,2,1,0:T(8,128)(2,1)S(1)}, bf16[1,1,96,128,128]{4,3,2,1,0:T(8,128)(2,1)}, u32[]{:S(2)}) copy-start(bf16[1,1,96,128,128]{4,3,2,1,0:T(8,128)(2,1)} %param.9) | copy-start | bytes 9437188
  29.6 35.0 %copy-start.2 = (bf16[1,1,32,128,128]{4,3,2,1,0:T(8,128)(2,1)S(1)}, bf16[1,1,32,128,128]{4,3,2,1,0:T(8,128)(2,1)}, u32[]{:S(2)}) copy-start(bf16[1,1,32,128,128]{4,3,2,1,0:T(8,128)(2,1)} %param.13) | copy-start | bytes 3145732
  29.6 35.0 %copy-start.3 = (bf16[1,1,32,8,128]{4,3,2,1,0:T(8,128)(2,1)S(1)}, bf16[1,1,32,8,128]{4,3,2,1,0:T(8,128)(2,1)}, u32[]{:S(2)}) copy-start(bf16[1,1,32,8,128]{4,3,2,1,0:T(8,128)(2,1)} %param.8) | copy-start | bytes 196612
  29.6 35.0 %copy-start.4 = (f32[1,1,128,128]{3,2,1,0:T(8,128)S(1)}, f32[1,1,128,128]{3,2,1,0:T(8,128)}, u32[]{:S(2)}) copy-start(f32[1,1,128,128]{3,2,1,0:T(8,128)} %param.14) | copy-start | bytes 196612
  29.6 35.0 %copy-start.5 = (f32[1,1,16,8,128]{4,3,2,1,0:T(8,128)S(1)}, f32[1,1,16,8,128]{4,3,2,1,0:T(8,128)}, u32[]{:S(2)}) copy-start(f32[1,1,16,8,128]{4,3,2,1,0:T(8,128)} %param.15) | copy-start | bytes 196612
  49.9 36.2 %all-to-all-start.2 = ((s16[8,136,128]{2,1,0:T(8,128)(2,1)}), s16[8,136,128]{2,1,0:T(8,128)(2,1)S(1)}, u32[]{:S(2)}, u32[]{:S(2)}) async-start(s16[8,136,128]{2,1,0:T(8,128)(2,1)} %merge.1), calls=%async_computation.2 | async-start | bytes 557056 | tf_op jit(solution)/shard_map/all_to_all | solution.py:190

commit v2 on v1

v2 whole, which is shorter than its diff:
```python
import jax
import jax.numpy as jnp
from jax import lax
from jax.experimental import pallas as pl
from jax.experimental.pallas import tpu as pltpu
from jax.sharding import Mesh, PartitionSpec as P

B = 128
E = 8
HIST = 32
K = 16
TPS = 6
GROUPS = 16
PANELS = 32
SLOTS = 96
ROWS = K * E
HALF = GROUPS // 2
PART = 4
NEAR = 4
NEXT = PANELS // NEAR
FULL = 32760.0

VMEM = pl.BlockSpec(memory_space=pltpu.VMEM)
SMEM = pl.BlockSpec(memory_space=pltpu.SMEM)
HBM = pl.BlockSpec(memory_space=pltpu.HBM)
HIGHEST = lax.Precision.HIGHEST


def dot(a, b):
    return jnp.dot(a, b, preferred_element_type=jnp.float32)


def encode(values):
    peak = jnp.maximum(jnp.max(jnp.abs(values), axis=0, keepdims=True), 1e-30)
    code = jnp.floor(jnp.log2(peak)) + 1.0
    scaled = jnp.round(values * (jnp.exp2(-code) * FULL)).astype(jnp.int32)
    return scaled.reshape(K, E, B).astype(jnp.int16), code


def decode(values, scale):
    return values.astype(jnp.int32).astype(jnp.float32).reshape(ROWS, B) * scale


def scales(codes):
    return jnp.exp2(codes.astype(jnp.int32).astype(jnp.float32)) * (1.0 / FULL)


def add_products(side, lists, tables, past, tiles, wide, total, slab, tile_sem, list_sem, begin):
    loads = [pltpu.make_async_copy(a, b, list_sem.at[i]) for i, (a, b) in enumerate(zip(lists, tables))]
    for load in loads:
        load.start()

    def tile_load(p):
        return pltpu.make_async_copy(tiles.at[pl.ds((2 * p + side) * TPS, TPS)], slab.at[p], tile_sem.at[p])

    for p in range(HALF):
        tile_load(p).start()
    wide[...] = past[...].astype(jnp.float32)
    begin()
    for load in loads:
        load.wait()
    lag, target, count = tables

    def sources(part, carry):
        these = [part * PART + i for i in range(PART)]
        for p in these:
            tile_load(p).wait()
        for p in these:
            h = 2 * p + side
            live = count[h]
            for j in range(TPS):
                s = h * TPS + j
                first = jnp.clip(HIST - lag[s], 0, HIST - K)
                place = jnp.where(j < live, jnp.clip(target[s], 0, PANELS - 1), PANELS)
                window = wide[p, pl.ds(first, K)].reshape(ROWS, B).astype(jnp.bfloat16)
                total[place] += dot(window, slab[p, j])
        return carry

    lax.fori_loop(0, HALF // PART, sources, 0)


def near_kernel(core, lag, target, count, tiles, past, total, *scratch):
    def begin():
        total[...] = jnp.zeros_like(total)

    wide, slab, tile_sem, list_sem, *tables = scratch
    add_products(core[0], (lag, target, count), tables, past, tiles, wide, total, slab, tile_sem, list_sem, begin)


def far_kernel(core, lag, target, count, tiles, past, before, out, *scratch):
    wide, slab, tile_sem, list_sem, *tables, total = scratch

    def begin():
        total[...] = before[...]

    add_products(1 - core[0], (lag, target, count), tables, past, tiles, wide, total, slab, tile_sem, list_sem, begin)

    def pack(d, carry):
        codes = []
        for z in range(NEXT):
            values, code = encode(total[z * NEAR + d])
            out[d, pl.ds(z * K, K)] = values
            codes.append(code)
        out[d, NEXT * K] = jnp.concatenate(codes, axis=0).astype(jnp.int32).astype(jnp.int16)
        return carry

    lax.fori_loop(0, NEAR, pack, 0)


def merge_kernel(got, out):
    scale = [scales(got[d, NEXT * K]) for d in range(NEAR)]
    for z in range(NEXT):
        value = decode(got[0, pl.ds(z * K, K)], scale[0][z : z + 1])
        for d in range(1, NEAR):
            value = value + decode(got[d, pl.ds(z * K, K)], scale[d][z : z + 1])
        values, code = encode(value)
        out[z, pl.ds(0, K)] = values
        wide = jnp.broadcast_to(code, (E, B)).astype(jnp.int32).astype(jnp.int16)
        out[z, K] = wide


def thirds(x):
    a = x.astype(jnp.bfloat16)
    rest = x - a.astype(jnp.float32)
    b = rest.astype(jnp.bfloat16)
    c = (rest - b.astype(jnp.float32)).astype(jnp.bfloat16)
    return a, b, c


def self_kernel(own_h, self_h, near_h, incident_h, base, steps, wide, own, self_tiles, near, incident, sem):
    pairs = ((own_h, own), (self_h, self_tiles), (near_h, near), (incident_h, incident))
    loads = [pltpu.make_async_copy(a, b, sem.at[i]) for i, (a, b) in enumerate(pairs)]
    for load in loads:
        load.start()
    for load in loads:
        load.wait()
    wide[pl.ds(0, HIST)] = own[...].astype(jnp.float32)
    wide[pl.ds(HIST, K)] = jnp.zeros((K, E, B), jnp.float32)
    drive = incident[...].reshape(ROWS, B)
    for lag in range(1, HIST + 1):
        window = wide[pl.ds(HIST - lag, K)].reshape(ROWS, B).astype(jnp.bfloat16)
        drive = drive - dot(window, self_tiles[lag - 1])
    base[...] = jnp.dot(drive, near[...], precision=HIGHEST, preferred_element_type=jnp.float32)
    a, b, c = thirds(near[...])
    for lag in range(1, K):
        tile = self_tiles[lag - 1]
        m = dot(tile, a) + dot(tile, b) + dot(tile, c)
        high = m.astype(jnp.bfloat16)
        steps[lag - 1, pl.ds(0, B)] = high
        steps[lag - 1, pl.ds(B, B)] = (m - high.astype(jnp.float32)).astype(jnp.bfloat16)


def solve_kernel(got, near, base, steps, density):
    far = decode(got[0, pl.ds(0, K)], scales(got[0, K])[0:1])
    for z in range(1, NEXT):
        far = far + decode(got[z, pl.ds(0, K)], scales(got[z, K])[0:1])
    drive = base[...] - jnp.dot(far, near[...], precision=HIGHEST, preferred_element_type=jnp.float32)
    rest = [drive[E * k : E * (k + 1)] for k in range(K)]
    for k in range(K):
        density[k] = rest[k]
        fresh = rest[k].astype(jnp.bfloat16)
        twice = jnp.concatenate([fresh, fresh], axis=1)
        for j in range(k + 1, K):
            rest[j] = rest[j] - dot(twice, steps[j - k - 1])


def keep(x):
    return pltpu.with_memory_space_constraint(x, pltpu.HBM)


def call(kernel, outs, in_specs, scratch=(), **kw):
    single = not isinstance(outs, (tuple, list))
    return pl.pallas_call(
        kernel,
        out_shape=outs,
        in_specs=in_specs,
        out_specs=VMEM if single else [VMEM] * len(outs),
        scratch_shapes=list(scratch),
        compiler_params=pltpu.CompilerParams(vmem_limit_bytes=24 << 20),
        cost_estimate=pl.CostEstimate(flops=kw["flops"], bytes_accessed=kw["bytes"], transcendentals=0),
        name=kw["name"],
    )


def local(history, tiles, tile_target, tile_lag, tile_count, self_tiles, near_inverse, incident):
    own = history[0, 0]
    core = lax.axis_index("core").astype(jnp.int32)[None]
    lists = tuple(keep(x[0, 0]) for x in (tile_lag, tile_target, tile_count))
    slot_tiles, near = keep(tiles[0, 0]), keep(near_inverse[0, 0])
    total = (PANELS + 1, ROWS, B)
    scratch = [
        pltpu.VMEM((HALF, HIST, E, B), jnp.float32),
        pltpu.VMEM((HALF, TPS, B, B), jnp.bfloat16),
        pltpu.SemaphoreType.DMA((HALF,)),
        pltpu.SemaphoreType.DMA((3,)),
        pltpu.SMEM((SLOTS,), jnp.int32),
        pltpu.SMEM((SLOTS,), jnp.int32),
        pltpu.SMEM((GROUPS,), jnp.int32),
    ]

    same = lax.all_to_all(jnp.broadcast_to(own, (HALF, HIST, E, B)), ("y_hi", "x"), 0, 0, tiled=True)
    other = lax.ppermute(same, "core", [(0, 1), (1, 0)])
    partial = call(
        near_kernel,
        jax.ShapeDtypeStruct(total, jnp.float32),
        [SMEM, HBM, HBM, HBM, HBM, VMEM],
        scratch,
        name="near",
        flops=48 << 22,
        bytes=4 << 20,
    )(core, *lists, slot_tiles, same)
    blocks = call(
        far_kernel,
        jax.ShapeDtypeStruct((NEAR, NEXT * K + 1, E, B), jnp.int16),
        [SMEM, HBM, HBM, HBM, HBM, VMEM, VMEM],
        scratch + [pltpu.VMEM(total, jnp.float32)],
        name="far",
        flops=48 << 22,
        bytes=6 << 20,
    )(core, *lists, slot_tiles, other, partial)
    got = lax.all_to_all(blocks, ("z_lo", "y_lo"), 0, 0, tiled=True)
    merged = call(
        merge_kernel,
        jax.ShapeDtypeStruct((NEXT, K + 1, E, B), jnp.int16),
        [VMEM],
        name="merge",
        flops=1 << 20,
        bytes=2 << 20,
    )(got)
    got = lax.all_to_all(merged, "z_hi", 0, 0, tiled=True)
    base, steps = call(
        self_kernel,
        [jax.ShapeDtypeStruct((ROWS, B), jnp.float32), jax.ShapeDtypeStruct((K - 1, 2 * B, B), jnp.bfloat16)],
        [HBM, HBM, HBM, HBM],
        [
            pltpu.VMEM((HIST + K, E, B), jnp.float32),
            pltpu.VMEM((HIST, E, B), jnp.bfloat16),
            pltpu.VMEM((HIST, B, B), jnp.bfloat16),
            pltpu.VMEM((B, B), jnp.float32),
            pltpu.VMEM((K, E, B), jnp.float32),
            pltpu.SemaphoreType.DMA((4,)),
        ],
        name="selfpast",
        flops=32 << 22,
        bytes=2 << 20,
    )(keep(own), keep(self_tiles[0, 0]), near, keep(incident[0, 0]))
    density = call(
        solve_kernel,
        jax.ShapeDtypeStruct((K, E, B), jnp.float32),
        [VMEM] * 4,
        name="solve",
        flops=16 << 22,
        bytes=2 << 20,
    )(got, near_inverse[0, 0], base, steps)
    return density[None, None]


def solution(mesh):
    fine = Mesh(mesh.devices.reshape(2, 4, 2, 8, 2, 2), ("y_hi", "x", "core", "z_hi", "z_lo", "y_lo"))
    row, col = ("y_hi", "x", "core"), ("z_hi", "z_lo", "y_lo")
    return jax.shard_map(
        local,
        mesh=fine,
        in_specs=(
            P(row, col, None, None, None),
            P(row, col, None, None, None),
            P(row, col, None),
            P(row, col, None),
            P(row, col, None),
            P(row, col, None, None, None),
            P(row, col, None, None),
            P(row, col, None, None, None),
        ),
        out_specs=P(row, col, None, None, None),
        check_vma=False,
    )
```

time: 89.3 us -> 84.2 us (0.943)
  the two profiles are of different devices: /device:TPU:8 before, /device:TPU:2 now
where the time goes in v2:
time: 84.2 us; the launch traced here: 83.8 us
  blocking collectives  36.1 us (43%)
  waiting for transfers between devices  19.2 us (23%)
  starting transfers between devices  16.7 us (20%)
  Pallas kernels  10.8 us (13%)
  local copies, waits for them, and re-layouts  0.91 us (1%)
    all_to_all x1, waiting for transfers between devices, local(): got = lax.all_to_all(merged, 'z_hi', 0, 0, tiled=True)  19.2 us
    all_to_all x1, blocking collectives, local(): got = lax.all_to_all(blocks, ('z_lo', 'y_lo'), 0, 0, tiled=True)  18.5 us
    all_to_all x1, blocking collectives, local(): lax.all_to_all(jnp.broadcast_to(own, (HALF, HIST, E, B)), ('y_hi', 'x'),...  17.7 us
    all_to_all x1, starting transfers between devices, local(): got = lax.all_to_all(merged, 'z_hi', 0, 0, tiled=True)  14.7 us
    pallas_call x1, Pallas kernels, local(): call(solve_kernel, jax.ShapeDtypeStruct((K, E, B), jnp.float32), [VMEM] *...  2.73 us
    pallas_call x1, Pallas kernels, local(): call(far_kernel, jax.ShapeDtypeStruct((NEAR, NEXT * K + 1, E, B), jnp.int...  2.55 us
    pallas_call x1, Pallas kernels, local(): call(self_kernel, [jax.ShapeDtypeStruct((ROWS, B), jnp.float32), jax.Shap...  2.3 us
    pallas_call x1, Pallas kernels, local(): call(near_kernel, jax.ShapeDtypeStruct(total, jnp.float32), [SMEM, HBM, H...  2.14 us
  transfers between devices with their start and end apart: 2, of which 1 were waited for; matrix products, arithmetic and copies ran while one was open for 0% of the time, Pallas kernels for 5%

profile of v2, /device:TPU:2, one launch (start us, length us, event | category | flops | bytes accessed | tf_op | source)
XLA Modules:
  0.0 83.8 jit_solution(17843723612777460028)
XLA Ops:
  0.0 0.9 %broadcast_in_dim.10 = bf16[8,32,8,128]{3,2,1,0:T(8,128)(2,1)S(1)} broadcast(bf16[32,8,128]{2,1,0:T(8,128)(2,1)} %bitcast.15), dimensions={1,2,3} | broadcast | bytes 589824 | tf_op jit(solution)/shard_map/broadcast_in_dim | solution.py:201
  0.9 17.7 %all_to_all.15.past = bf16[8,32,8,128]{3,2,1,0:T(8,128)(2,1)S(1)} all-to-all(bf16[8,32,8,128]{3,2,1,0:T(8,128)(2,1)S(1)} %broadcast_in_dim.10), channel_id=1, replica_groups=mesh['y_hi'=2,'x'=4,'core'=2,'z_hi'=8,'z_lo'=2,'y_lo'=2] {'y_hi','x'}, dimensions={0} | all-to-all | bytes 1048576 | tf_op jit(solution)/shard_map/all_to_all | solution.py:201
  18.6 1.9 %collective-permute-start = (bf16[8,32,8,128]{3,2,1,0:T(8,128)(2,1)S(1)}, bf16[8,32,8,128]{3,2,1,0:T(8,128)(2,1)S(1)}, u32[]{:S(2)}, u32[]{:S(2)}) collective-permute-start(bf16[8,32,8,128]{3,2,1,0:T(8,128)(2,1)S(1)} %all_to_all.15.past), channel_id=1, source_target_pairs={{0,32},{32,0},{1,33},{33,1},{2,34},{34,2},{3,35},{35,3},{4,36},{36... | collective-permute-start | bytes 1572872 | tf_op jit(solution)/shard_map/ppermute | solution.py:202
  20.5 2.1 %near.1.before = f32[33,128,128]{2,1,0:T(8,128)S(1)} custom-call(s32[1]{0:T(128)} %bitcast.core, s32[96]{0:T(128)} %bitcast.18, s32[96]{0:T(128)} %bitcast.20, s32[16]{0:T(128)} %bitcast.22, bf16[96,128,128]{2,1,0:T(8,128)(2,1)} %bitcast.12, bf16[8,32,8,128]{3,2,1,0:T(8,128)(2,1)S(1)} %all_to_all.15.past), custom_call_target="tpu_custom_call" | custom-call | flops 201326592 | bytes 4194304 | tf_op jit(solution)/shard_map/near/pallas_call | solution.py:203
  22.7 0.0 collective-permute-done.past
  22.7 2.5 %far.1 = s16[4,129,8,128]{3,2,1,0:T(8,128)(2,1)S(1)} custom-call(s32[1]{0:T(128)} %bitcast.core, s32[96]{0:T(128)} %bitcast.19, s32[96]{0:T(128)} %bitcast.21, s32[16]{0:T(128)} %bitcast.23, bf16[96,128,128]{2,1,0:T(8,128)(2,1)} %bitcast.13, bf16[8,32,8,128]{3,2,1,0:T(8,128)(2,1)S(1)} %collective-permute-done.past, f32[33,128,128]{2,1,0:T(8,128)S(1)} %near.1.before), custom_call_target="tpu_custom_call" | custom-call | flops 201326592 | bytes 6291456 | tf_op jit(solution)/shard_map/far/pallas_call | solution.py:212
  25.2 0.0 copy-start
  25.2 18.5 %all_to_all.16.got = s16[4,129,8,128]{3,2,1,0:T(8,128)(2,1)S(1)} all-to-all(s16[4,129,8,128]{3,2,1,0:T(8,128)(2,1)S(1)} %far.1), channel_id=1, replica_groups=mesh['y_hi'=2,'x'=4,'core'=2,'z_hi'=8,'z_lo'=2,'y_lo'=2] {'z_lo','y_lo'}, dimensions={0} | all-to-all | bytes 2113536 | tf_op jit(solution)/shard_map/all_to_all | solution.py:221
  43.7 1.1 %merge.1 = s16[8,17,8,128]{3,2,1,0:T(8,128)(2,1)} custom-call(s16[4,129,8,128]{3,2,1,0:T(8,128)(2,1)S(1)} %all_to_all.16.got), custom_call_target="tpu_custom_call" | custom-call | flops 1048576 | bytes 2097152 | tf_op jit(solution)/shard_map/merge/pallas_call | solution.py:222
  44.8 14.7 %all-to-all-start.2 = ((s16[8,17,8,128]{3,2,1,0:T(8,128)(2,1)}), s16[8,17,8,128]{3,2,1,0:T(8,128)(2,1)S(1)}, u32[]{:S(2)}, u32[]{:S(2)}) async-start(s16[8,17,8,128]{3,2,1,0:T(8,128)(2,1)} %merge.1), calls=%async_computation.2 | async-start | bytes 557056 | tf_op jit(solution)/shard_map/all_to_all | solution.py:230
  59.5 2.3 %selfpast.1 = (f32[128,128]{1,0:T(8,128)S(1)}, bf16[15,256,128]{2,1,0:T(8,128)(2,1)S(1)}) custom-call(bf16[32,8,128]{2,1,0:T(8,128)(2,1)} %bitcast.16, bf16[32,128,128]{2,1,0:T(8,128)(2,1)} %bitcast.14, f32[128,128]{1,0:T(8,128)} %bitcast.10, f32[16,8,128]{2,1,0:T(8,128)} %bitcast.17), custom_call_target="tpu_custom_call" | custom-call | flops 134217728 | bytes 2097152 | tf_op jit(solution)/shard_map/selfpast/pallas_call | solution.py:231
  61.8 19.2 %all-to-all-done.2.got = s16[8,17,8,128]{3,2,1,0:T(8,128)(2,1)S(1)} async-done(((s16[8,17,8,128]{3,2,1,0:T(8,128)(2,1)}), s16[8,17,8,128]{3,2,1,0:T(8,128)(2,1)S(1)}, u32[]{:S(2)}, u32[]{:S(2)}) %all-to-all-start.2) | async-done | bytes 278560 | tf_op jit(solution)/shard_map/all_to_all | solution.py:230
  81.0 0.0 copy-done
  81.0 2.7 %solve.1 = f32[16,8,128]{2,1,0:T(8,128)} custom-call(s16[8,17,8,128]{3,2,1,0:T(8,128)(2,1)S(1)} %all-to-all-done.2.got, f32[128,128]{1,0:T(8,128)S(1)} %bitcast.11, f32[128,128]{1,0:T(8,128)S(1)} %get-tuple-element.7.base, bf16[15,256,128]{2,1,0:T(8,128)(2,1)S(1)} %get-tuple-element.8.steps), custom_call_target="tpu_custom_call" | custom-call | flops 67108864 | bytes 2097152 | tf_op jit(solution)/shard_map/solve/pallas_call | solution.py:247
Async XLA Ops:
  18.6 4.1 %collective-permute-start = (bf16[8,32,8,128]{3,2,1,0:T(8,128)(2,1)S(1)}, bf16[8,32,8,128]{3,2,1,0:T(8,128)(2,1)S(1)}, u32[]{:S(2)}, u32[]{:S(2)}) collective-permute-start(bf16[8,32,8,128]{3,2,1,0:T(8,128)(2,1)S(1)} %all_to_all.15.past), channel_id=1, source_target_pairs={{0,32},{32,0},{1,33},{33,1},{2,34},{34,2},{3,35},{35,3},{4,36},{36... | collective-permute-start | bytes 1572872 | tf_op jit(solution)/shard_map/ppermute | solution.py:202
  25.2 55.8 %copy-start = (f32[1,1,128,128]{3,2,1,0:T(8,128)S(1)}, f32[1,1,128,128]{3,2,1,0:T(8,128)}, u32[]{:S(2)}) copy-start(f32[1,1,128,128]{3,2,1,0:T(8,128)} %param.14) | copy-start | bytes 196612
  44.8 36.3 %all-to-all-start.2 = ((s16[8,17,8,128]{3,2,1,0:T(8,128)(2,1)}), s16[8,17,8,128]{3,2,1,0:T(8,128)(2,1)S(1)}, u32[]{:S(2)}, u32[]{:S(2)}) async-start(s16[8,17,8,128]{3,2,1,0:T(8,128)(2,1)} %merge.1), calls=%async_computation.2 | async-start | bytes 557056 | tf_op jit(solution)/shard_map/all_to_all | solution.py:230

commit v3 on v2

--- a/solution.py
+++ b/solution.py
@@ -19,6 +19,8 @@
 NEAR = 4
 NEXT = PANELS // NEAR
 FULL = 32760.0
+NEAR_GROUPS = [[NEAR * s + d for d in range(NEAR)] for s in range(NEXT)]
+NEXT_GROUPS = [[NEAR * s + (d ^ (2 * (s >= NEXT // 2))) for s in range(NEXT)] for d in range(NEAR)]
 
 VMEM = pl.BlockSpec(memory_space=pltpu.VMEM)
 SMEM = pl.BlockSpec(memory_space=pltpu.SMEM)
@@ -87,7 +89,7 @@
     add_products(core[0], (lag, target, count), tables, past, tiles, wide, total, slab, tile_sem, list_sem, begin)
 
 
-def far_kernel(core, lag, target, count, tiles, past, before, out, *scratch):
+def far_kernel(core, far_half, lag, target, count, tiles, past, before, out, *scratch):
     wide, slab, tile_sem, list_sem, *tables, total = scratch
 
     def begin():
@@ -98,7 +100,8 @@
     def pack(d, carry):
         codes = []
         for z in range(NEXT):
-            values, code = encode(total[z * NEAR + d])
+            swap = far_half[0] ^ (z >= NEXT // 2)
+            values, code = encode(total[z * NEAR + (d ^ (2 * swap))])
             out[d, pl.ds(z * K, K)] = values
             codes.append(code)
         out[d, NEXT * K] = jnp.concatenate(codes, axis=0).astype(jnp.int32).astype(jnp.int16)
@@ -185,6 +188,7 @@
 def local(history, tiles, tile_target, tile_lag, tile_count, self_tiles, near_inverse, incident):
     own = history[0, 0]
     core = lax.axis_index("core").astype(jnp.int32)[None]
+    far_half = (lax.axis_index("col") >= PANELS // 2).astype(jnp.int32)[None]
     lists = tuple(keep(x[0, 0]) for x in (tile_lag, tile_target, tile_count))
     slot_tiles, near = keep(tiles[0, 0]), keep(near_inverse[0, 0])
     total = (PANELS + 1, ROWS, B)
@@ -212,13 +216,13 @@
     blocks = call(
         far_kernel,
         jax.ShapeDtypeStruct((NEAR, NEXT * K + 1, E, B), jnp.int16),
-        [SMEM, HBM, HBM, HBM, HBM, VMEM, VMEM],
+        [SMEM, SMEM, HBM, HBM, HBM, HBM, VMEM, VMEM],
         scratch + [pltpu.VMEM(total, jnp.float32)],
         name="far",
         flops=48 << 22,
         bytes=6 << 20,
-    )(core, *lists, slot_tiles, other, partial)
-    got = lax.all_to_all(blocks, ("z_lo", "y_lo"), 0, 0, tiled=True)
+    )(core, far_half, *lists, slot_tiles, other, partial)
+    got = lax.all_to_all(blocks, "col", 0, 0, tiled=True, axis_index_groups=NEAR_GROUPS)
     merged = call(
         merge_kernel,
         jax.ShapeDtypeStruct((NEXT, K + 1, E, B), jnp.int16),
@@ -227,7 +231,7 @@
         flops=1 << 20,
         bytes=2 << 20,
     )(got)
-    got = lax.all_to_all(merged, "z_hi", 0, 0, tiled=True)
+    got = lax.all_to_all(merged, "col", 0, 0, tiled=True, axis_index_groups=NEXT_GROUPS)
     base, steps = call(
         self_kernel,
         [jax.ShapeDtypeStruct((ROWS, B), jnp.float32), jax.ShapeDtypeStruct((K - 1, 2 * B, B), jnp.bfloat16)],
@@ -256,8 +260,8 @@
 
 
 def solution(mesh):
-    fine = Mesh(mesh.devices.reshape(2, 4, 2, 8, 2, 2), ("y_hi", "x", "core", "z_hi", "z_lo", "y_lo"))
-    row, col = ("y_hi", "x", "core"), ("z_hi", "z_lo", "y_lo")
+    fine = Mesh(mesh.devices.reshape(2, 4, 2, PANELS), ("y_hi", "x", "core", "col"))
+    row, col = ("y_hi", "x", "core"), "col"
     return jax.shard_map(
         local,
         mesh=fine,

time: 84.2 us -> 82.6 us (0.981)
  the two profiles are of different devices: /device:TPU:2 before, /device:TPU:32 now
where the time goes in v3:
time: 82.6 us; the launch traced here: 82 us
  blocking collectives  35.4 us (43%)
  waiting for transfers between devices  18.2 us (22%)
  starting transfers between devices  16.6 us (20%)
  Pallas kernels  10.8 us (13%)
  local copies, waits for them, and re-layouts  0.91 us (1%)
    all_to_all x1, blocking collectives, local(): lax.all_to_all(jnp.broadcast_to(own, (HALF, HIST, E, B)), ('y_hi', 'x'),...  18.3 us
    all_to_all x1, waiting for transfers between devices, local(): lax.all_to_all(merged, 'col', 0, 0, tiled=True, axis_index_groups=NEXT_GR...  18.2 us
    all_to_all x1, blocking collectives, local(): lax.all_to_all(blocks, 'col', 0, 0, tiled=True, axis_index_groups=NEAR_GR...  17.1 us
    all_to_all x1, starting transfers between devices, local(): lax.all_to_all(merged, 'col', 0, 0, tiled=True, axis_index_groups=NEXT_GR...  14.7 us
    pallas_call x1, Pallas kernels, local(): call(solve_kernel, jax.ShapeDtypeStruct((K, E, B), jnp.float32), [VMEM] *...  2.73 us
    pallas_call x1, Pallas kernels, local(): call(far_kernel, jax.ShapeDtypeStruct((NEAR, NEXT * K + 1, E, B), jnp.int...  2.54 us
    pallas_call x1, Pallas kernels, local(): call(self_kernel, [jax.ShapeDtypeStruct((ROWS, B), jnp.float32), jax.Shap...  2.3 us
    pallas_call x1, Pallas kernels, local(): call(near_kernel, jax.ShapeDtypeStruct(total, jnp.float32), [SMEM, HBM, H...  2.15 us
  transfers between devices with their start and end apart: 2, of which 1 were waited for; matrix products, arithmetic and copies ran while one was open for 0% of the time, Pallas kernels for 5%

profile of v3, /device:TPU:32, one launch (start us, length us, event | category | flops | bytes accessed | tf_op | source)
XLA Modules:
  0.0 82.0 jit_solution(13113654009323772589)
XLA Ops:
  0.0 0.9 %broadcast_in_dim.17 = bf16[8,32,8,128]{3,2,1,0:T(8,128)(2,1)S(1)} broadcast(bf16[32,8,128]{2,1,0:T(8,128)(2,1)} %bitcast.16), dimensions={1,2,3} | broadcast | bytes 589824 | tf_op jit(solution)/shard_map/broadcast_in_dim | solution.py:205
  0.9 18.3 %all_to_all.15.past = bf16[8,32,8,128]{3,2,1,0:T(8,128)(2,1)S(1)} all-to-all(bf16[8,32,8,128]{3,2,1,0:T(8,128)(2,1)S(1)} %broadcast_in_dim.17), channel_id=1, replica_groups=mesh['y_hi'=2,'x'=4,'core'=2,'col'=32] {'y_hi','x'}, dimensions={0} | all-to-all | bytes 1048576 | tf_op jit(solution)/shard_map/all_to_all | solution.py:205
  19.2 1.9 %collective-permute-start = (bf16[8,32,8,128]{3,2,1,0:T(8,128)(2,1)S(1)}, bf16[8,32,8,128]{3,2,1,0:T(8,128)(2,1)S(1)}, u32[]{:S(2)}, u32[]{:S(2)}) collective-permute-start(bf16[8,32,8,128]{3,2,1,0:T(8,128)(2,1)S(1)} %all_to_all.15.past), channel_id=1, source_target_pairs={{0,32},{32,0},{1,33},{33,1},{2,34},{34,2},{3,35},{35,3},{4,36},{36... | collective-permute-start | bytes 1572872 | tf_op jit(solution)/shard_map/ppermute | solution.py:206
  21.1 2.1 %near.1.before = f32[33,128,128]{2,1,0:T(8,128)S(1)} custom-call(s32[1]{0:T(128)} %bitcast.core, s32[96]{0:T(128)} %bitcast.19, s32[96]{0:T(128)} %bitcast.21, s32[16]{0:T(128)} %bitcast.23, bf16[96,128,128]{2,1,0:T(8,128)(2,1)} %bitcast.13, bf16[8,32,8,128]{3,2,1,0:T(8,128)(2,1)S(1)} %all_to_all.15.past), custom_call_target="tpu_custom_call" | custom-call | flops 201326592 | bytes 4194304 | tf_op jit(solution)/shard_map/near/pallas_call | solution.py:207
  23.3 0.0 collective-permute-done.past
  23.3 2.5 %far.1 = s16[4,129,8,128]{3,2,1,0:T(8,128)(2,1)S(1)} custom-call(s32[1]{0:T(128)} %bitcast.core, s32[1]{0:T(128)} %bitcast.1.far_half, s32[96]{0:T(128)} %bitcast.20, s32[96]{0:T(128)} %bitcast.22, s32[16]{0:T(128)} %bitcast.24, bf16[96,128,128]{2,1,0:T(8,128)(2,1)} %bitcast.14, bf16[8,32,8,128]{3,2,1,0:T(8,128)(2,1)S(1)} %collective-permute-done.past, ...), custom_call_target="tpu_custom_call" | custom-call | flops 201326592 | bytes 6291456 | tf_op jit(solution)/shard_map/far/pallas_call | solution.py:216
  25.9 0.0 copy-start
  25.9 17.1 %all_to_all.16.got = s16[4,129,8,128]{3,2,1,0:T(8,128)(2,1)S(1)} all-to-all(s16[4,129,8,128]{3,2,1,0:T(8,128)(2,1)S(1)} %far.1), channel_id=1, replica_groups={{0,1,2,3},{4,5,6,7},{8,9,10,11},{12,13,14,15},{16,17,18,19},{20,21,22,2..., dimensions={0} | all-to-all | bytes 2113536 | tf_op jit(solution)/shard_map/all_to_all | solution.py:225
  43.0 1.1 %merge.1 = s16[8,17,8,128]{3,2,1,0:T(8,128)(2,1)} custom-call(s16[4,129,8,128]{3,2,1,0:T(8,128)(2,1)S(1)} %all_to_all.16.got), custom_call_target="tpu_custom_call" | custom-call | flops 1048576 | bytes 2097152 | tf_op jit(solution)/shard_map/merge/pallas_call | solution.py:226
  44.1 14.7 %all-to-all-start.2 = ((s16[8,17,8,128]{3,2,1,0:T(8,128)(2,1)}), s16[8,17,8,128]{3,2,1,0:T(8,128)(2,1)S(1)}, u32[]{:S(2)}, u32[]{:S(2)}) async-start(s16[8,17,8,128]{3,2,1,0:T(8,128)(2,1)} %merge.1), calls=%async_computation.2 | async-start | bytes 557056 | tf_op jit(solution)/shard_map/all_to_all | solution.py:234
  58.7 2.3 %selfpast.1 = (f32[128,128]{1,0:T(8,128)S(1)}, bf16[15,256,128]{2,1,0:T(8,128)(2,1)S(1)}) custom-call(bf16[32,8,128]{2,1,0:T(8,128)(2,1)} %bitcast.17, bf16[32,128,128]{2,1,0:T(8,128)(2,1)} %bitcast.15, f32[128,128]{1,0:T(8,128)} %bitcast.11, f32[16,8,128]{2,1,0:T(8,128)} %bitcast.18), custom_call_target="tpu_custom_call" | custom-call | flops 134217728 | bytes 2097152 | tf_op jit(solution)/shard_map/selfpast/pallas_call | solution.py:235
  61.1 18.2 %all-to-all-done.2.got = s16[8,17,8,128]{3,2,1,0:T(8,128)(2,1)S(1)} async-done(((s16[8,17,8,128]{3,2,1,0:T(8,128)(2,1)}), s16[8,17,8,128]{3,2,1,0:T(8,128)(2,1)S(1)}, u32[]{:S(2)}, u32[]{:S(2)}) %all-to-all-start.2) | async-done | bytes 278560 | tf_op jit(solution)/shard_map/all_to_all | solution.py:234
  79.3 0.0 copy-done
  79.3 2.7 %solve.1 = f32[16,8,128]{2,1,0:T(8,128)} custom-call(s16[8,17,8,128]{3,2,1,0:T(8,128)(2,1)S(1)} %all-to-all-done.2.got, f32[128,128]{1,0:T(8,128)S(1)} %bitcast.12, f32[128,128]{1,0:T(8,128)S(1)} %get-tuple-element.7.base, bf16[15,256,128]{2,1,0:T(8,128)(2,1)S(1)} %get-tuple-element.8.steps), custom_call_target="tpu_custom_call" | custom-call | flops 67108864 | bytes 2097152 | tf_op jit(solution)/shard_map/solve/pallas_call | solution.py:251
Async XLA Ops:
  19.2 4.1 %collective-permute-start = (bf16[8,32,8,128]{3,2,1,0:T(8,128)(2,1)S(1)}, bf16[8,32,8,128]{3,2,1,0:T(8,128)(2,1)S(1)}, u32[]{:S(2)}, u32[]{:S(2)}) collective-permute-start(bf16[8,32,8,128]{3,2,1,0:T(8,128)(2,1)S(1)} %all_to_all.15.past), channel_id=1, source_target_pairs={{0,32},{32,0},{1,33},{33,1},{2,34},{34,2},{3,35},{35,3},{4,36},{36... | collective-permute-start | bytes 1572872 | tf_op jit(solution)/shard_map/ppermute | solution.py:206
  25.9 53.4 %copy-start = (f32[1,1,128,128]{3,2,1,0:T(8,128)S(1)}, f32[1,1,128,128]{3,2,1,0:T(8,128)}, u32[]{:S(2)}) copy-start(f32[1,1,128,128]{3,2,1,0:T(8,128)} %param.14) | copy-start | bytes 196612
  44.1 35.2 %all-to-all-start.2 = ((s16[8,17,8,128]{3,2,1,0:T(8,128)(2,1)}), s16[8,17,8,128]{3,2,1,0:T(8,128)(2,1)S(1)}, u32[]{:S(2)}, u32[]{:S(2)}) async-start(s16[8,17,8,128]{3,2,1,0:T(8,128)(2,1)} %merge.1), calls=%async_computation.2 | async-start | bytes 557056 | tf_op jit(solution)/shard_map/all_to_all | solution.py:234

commit v4 on v3

--- a/solution.py
+++ b/solution.py
@@ -18,9 +18,16 @@
 PART = 4
 NEAR = 4
 NEXT = PANELS // NEAR
+UNITS = K // 2
 FULL = 32760.0
-NEAR_GROUPS = [[NEAR * s + d for d in range(NEAR)] for s in range(NEXT)]
-NEXT_GROUPS = [[NEAR * s + (d ^ (2 * (s >= NEXT // 2))) for s in range(NEXT)] for d in range(NEAR)]
+NEAR_GROUPS = [
+    [PANELS * c + (NEAR * s + d + 2 * c) % PANELS for d in range(NEAR)] for c in range(2) for s in range(NEXT)
+]
+NEXT_GROUPS = [
+    [PANELS * c + (NEAR * s + (d ^ (2 * (s >= NEXT // 2))) + 2 * c) % PANELS for s in range(NEXT)]
+    for c in range(2)
+    for d in range(NEAR)
+]
 
 VMEM = pl.BlockSpec(memory_space=pltpu.VMEM)
 SMEM = pl.BlockSpec(memory_space=pltpu.SMEM)
@@ -36,7 +43,7 @@
     peak = jnp.maximum(jnp.max(jnp.abs(values), axis=0, keepdims=True), 1e-30)
     code = jnp.floor(jnp.log2(peak)) + 1.0
     scaled = jnp.round(values * (jnp.exp2(-code) * FULL)).astype(jnp.int32)
-    return scaled.reshape(K, E, B).astype(jnp.int16), code
+    return scaled, code
 
 
 def decode(values, scale):
@@ -101,23 +108,25 @@
         codes = []
         for z in range(NEXT):
             swap = far_half[0] ^ (z >= NEXT // 2)
-            values, code = encode(total[z * NEAR + (d ^ (2 * swap))])
-            out[d, pl.ds(z * K, K)] = values
+            place = z * NEAR + (d ^ (2 * swap)) + 2 * core[0]
+            values, code = encode(total[lax.rem(place, PANELS)])
+            out[d, pl.ds(z * UNITS, UNITS)] = values.reshape(UNITS, 2 * E, B).astype(jnp.int16)
             codes.append(code)
-        out[d, NEXT * K] = jnp.concatenate(codes, axis=0).astype(jnp.int32).astype(jnp.int16)
+        rows = jnp.concatenate(codes + codes, axis=0)
+        out[d, NEXT * UNITS] = rows.astype(jnp.int32).astype(jnp.int16)
         return carry
 
     lax.fori_loop(0, NEAR, pack, 0)
 
 
 def merge_kernel(got, out):
-    scale = [scales(got[d, NEXT * K]) for d in range(NEAR)]
+    scale = [scales(got[d, NEXT * UNITS]) for d in range(NEAR)]
     for z in range(NEXT):
-        value = decode(got[0, pl.ds(z * K, K)], scale[0][z : z + 1])
+        value = decode(got[0, pl.ds(z * UNITS, UNITS)], scale[0][z : z + 1])
         for d in range(1, NEAR):
-            value = value + decode(got[d, pl.ds(z * K, K)], scale[d][z : z + 1])
+            value = value + decode(got[d, pl.ds(z * UNITS, UNITS)], scale[d][z : z + 1])
         values, code = encode(value)
-        out[z, pl.ds(0, K)] = values
+        out[z, pl.ds(0, K)] = values.reshape(K, E, B).astype(jnp.int16)
         wide = jnp.broadcast_to(code, (E, B)).astype(jnp.int32).astype(jnp.int16)
         out[z, K] = wide
 
@@ -187,8 +196,10 @@
 
 def local(history, tiles, tile_target, tile_lag, tile_count, self_tiles, near_inverse, incident):
     own = history[0, 0]
-    core = lax.axis_index("core").astype(jnp.int32)[None]
-    far_half = (lax.axis_index("col") >= PANELS // 2).astype(jnp.int32)[None]
+    side = lax.axis_index("core").astype(jnp.int32)
+    core = side[None]
+    place = (lax.axis_index("col").astype(jnp.int32) + PANELS - 2 * side) % PANELS
+    far_half = (place >= PANELS // 2).astype(jnp.int32)[None]
     lists = tuple(keep(x[0, 0]) for x in (tile_lag, tile_target, tile_count))
     slot_tiles, near = keep(tiles[0, 0]), keep(near_inverse[0, 0])
     total = (PANELS + 1, ROWS, B)
@@ -215,14 +226,14 @@
     )(core, *lists, slot_tiles, same)
     blocks = call(
         far_kernel,
-        jax.ShapeDtypeStruct((NEAR, NEXT * K + 1, E, B), jnp.int16),
+        jax.ShapeDtypeStruct((NEAR, NEXT * UNITS + 1, 2 * E, B), jnp.int16),
         [SMEM, SMEM, HBM, HBM, HBM, HBM, VMEM, VMEM],
         scratch + [pltpu.VMEM(total, jnp.float32)],
         name="far",
         flops=48 << 22,
         bytes=6 << 20,
     )(core, far_half, *lists, slot_tiles, other, partial)
-    got = lax.all_to_all(blocks, "col", 0, 0, tiled=True, axis_index_groups=NEAR_GROUPS)
+    got = lax.all_to_all(blocks, ("core", "col"), 0, 0, tiled=True, axis_index_groups=NEAR_GROUPS)
     merged = call(
         merge_kernel,
         jax.ShapeDtypeStruct((NEXT, K + 1, E, B), jnp.int16),
@@ -231,7 +242,7 @@
         flops=1 << 20,
         bytes=2 << 20,
     )(got)
-    got = lax.all_to_all(merged, "col", 0, 0, tiled=True, axis_index_groups=NEXT_GROUPS)
+    got = lax.all_to_all(merged, ("core", "col"), 0, 0, tiled=True, axis_index_groups=NEXT_GROUPS)
     base, steps = call(
         self_kernel,
         [jax.ShapeDtypeStruct((ROWS, B), jnp.float32), jax.ShapeDtypeStruct((K - 1, 2 * B, B), jnp.bfloat16)],

time: 82.6 us -> 82.9 us (level)
  the two profiles are of different devices: /device:TPU:32 before, /device:TPU:2 now
where the time goes in v4:
time: 82.9 us; the launch traced here: 82.4 us
  blocking collectives  31.3 us (38%)
  starting transfers between devices  20.2 us (24%)
  waiting for transfers between devices  19.1 us (23%)
  Pallas kernels  10.8 us (13%)
  local copies, waits for them, and re-layouts  0.91 us (1%)
    all_to_all x1, waiting for transfers between devices, local(): lax.all_to_all(merged, ('core', 'col'), 0, 0, tiled=True, axis_index_grou...  19.1 us
    all_to_all x1, starting transfers between devices, local(): lax.all_to_all(merged, ('core', 'col'), 0, 0, tiled=True, axis_index_grou...  18.3 us
    all_to_all x1, blocking collectives, local(): lax.all_to_all(jnp.broadcast_to(own, (HALF, HIST, E, B)), ('y_hi', 'x'),...  17.7 us
    all_to_all x1, blocking collectives, local(): lax.all_to_all(blocks, ('core', 'col'), 0, 0, tiled=True, axis_index_grou...  13.6 us
    pallas_call x1, Pallas kernels, local(): call(solve_kernel, jax.ShapeDtypeStruct((K, E, B), jnp.float32), [VMEM] *...  2.73 us
    pallas_call x1, Pallas kernels, local(): call(far_kernel, jax.ShapeDtypeStruct((NEAR, NEXT * UNITS + 1, 2 * E, B),...  2.56 us
    pallas_call x1, Pallas kernels, local(): call(self_kernel, [jax.ShapeDtypeStruct((ROWS, B), jnp.float32), jax.Shap...  2.31 us
    pallas_call x1, Pallas kernels, local(): call(near_kernel, jax.ShapeDtypeStruct(total, jnp.float32), [SMEM, HBM, H...  2.14 us
  transfers between devices with their start and end apart: 2, of which 1 were waited for; matrix products, arithmetic and copies ran while one was open for 0% of the time, Pallas kernels for 5%

profile of v4, /device:TPU:2, one launch (start us, length us, event | category | flops | bytes accessed | tf_op | source)
XLA Modules:
  0.0 82.4 jit_solution(9829960096385580342)
XLA Ops:
  0.0 0.9 %broadcast_in_dim.17 = bf16[8,32,8,128]{3,2,1,0:T(8,128)(2,1)S(1)} broadcast(bf16[32,8,128]{2,1,0:T(8,128)(2,1)} %bitcast.16), dimensions={1,2,3} | broadcast | bytes 589824 | tf_op jit(solution)/shard_map/broadcast_in_dim | solution.py:216
  0.9 17.7 %all_to_all.15.past = bf16[8,32,8,128]{3,2,1,0:T(8,128)(2,1)S(1)} all-to-all(bf16[8,32,8,128]{3,2,1,0:T(8,128)(2,1)S(1)} %broadcast_in_dim.17), channel_id=1, replica_groups=mesh['y_hi'=2,'x'=4,'core'=2,'col'=32] {'y_hi','x'}, dimensions={0} | all-to-all | bytes 1048576 | tf_op jit(solution)/shard_map/all_to_all | solution.py:216
  18.6 1.9 %collective-permute-start = (bf16[8,32,8,128]{3,2,1,0:T(8,128)(2,1)S(1)}, bf16[8,32,8,128]{3,2,1,0:T(8,128)(2,1)S(1)}, u32[]{:S(2)}, u32[]{:S(2)}) collective-permute-start(bf16[8,32,8,128]{3,2,1,0:T(8,128)(2,1)S(1)} %all_to_all.15.past), channel_id=1, source_target_pairs={{0,32},{32,0},{1,33},{33,1},{2,34},{34,2},{3,35},{35,3},{4,36},{36... | collective-permute-start | bytes 1572872 | tf_op jit(solution)/shard_map/ppermute | solution.py:217
  20.5 2.1 %near.1.before = f32[33,128,128]{2,1,0:T(8,128)S(1)} custom-call(s32[1]{0:T(128)} %bitcast.core, s32[96]{0:T(128)} %bitcast.19, s32[96]{0:T(128)} %bitcast.21, s32[16]{0:T(128)} %bitcast.23, bf16[96,128,128]{2,1,0:T(8,128)(2,1)} %bitcast.13, bf16[8,32,8,128]{3,2,1,0:T(8,128)(2,1)S(1)} %all_to_all.15.past), custom_call_target="tpu_custom_call" | custom-call | flops 201326592 | bytes 4194304 | tf_op jit(solution)/shard_map/near/pallas_call | solution.py:218
  22.7 0.0 collective-permute-done.past
  22.7 2.6 %far.1 = s16[4,65,16,128]{3,2,1,0:T(8,128)(2,1)S(1)} custom-call(s32[1]{0:T(128)} %bitcast.core, s32[1]{0:T(128)} %bitcast.1.far_half, s32[96]{0:T(128)} %bitcast.20, s32[96]{0:T(128)} %bitcast.22, s32[16]{0:T(128)} %bitcast.24, bf16[96,128,128]{2,1,0:T(8,128)(2,1)} %bitcast.14, bf16[8,32,8,128]{3,2,1,0:T(8,128)(2,1)S(1)} %collective-permute-done.past, ...), custom_call_target="tpu_custom_call" | custom-call | flops 201326592 | bytes 6291456 | tf_op jit(solution)/shard_map/far/pallas_call | solution.py:227
  25.2 0.0 copy-start
  25.3 13.6 %all_to_all.16.got = s16[4,65,16,128]{3,2,1,0:T(8,128)(2,1)S(1)} all-to-all(s16[4,65,16,128]{3,2,1,0:T(8,128)(2,1)S(1)} %far.1), channel_id=1, replica_groups={{0,1,2,3},{4,5,6,7},{8,9,10,11},{12,13,14,15},{16,17,18,19},{20,21,22,2..., dimensions={0} | all-to-all | bytes 2129920 | tf_op jit(solution)/shard_map/all_to_all | solution.py:236
  38.9 1.1 %merge.1 = s16[8,17,8,128]{3,2,1,0:T(8,128)(2,1)} custom-call(s16[4,65,16,128]{3,2,1,0:T(8,128)(2,1)S(1)} %all_to_all.16.got), custom_call_target="tpu_custom_call" | custom-call | flops 1048576 | bytes 2097152 | tf_op jit(solution)/shard_map/merge/pallas_call | solution.py:237
  39.9 18.3 %all-to-all-start.2 = ((s16[8,17,8,128]{3,2,1,0:T(8,128)(2,1)}), s16[8,17,8,128]{3,2,1,0:T(8,128)(2,1)S(1)}, u32[]{:S(2)}, u32[]{:S(2)}) async-start(s16[8,17,8,128]{3,2,1,0:T(8,128)(2,1)} %merge.1), calls=%async_computation.2 | async-start | bytes 557056 | tf_op jit(solution)/shard_map/all_to_all | solution.py:245
  58.3 2.3 %selfpast.1 = (f32[128,128]{1,0:T(8,128)S(1)}, bf16[15,256,128]{2,1,0:T(8,128)(2,1)S(1)}) custom-call(bf16[32,8,128]{2,1,0:T(8,128)(2,1)} %bitcast.17, bf16[32,128,128]{2,1,0:T(8,128)(2,1)} %bitcast.15, f32[128,128]{1,0:T(8,128)} %bitcast.11, f32[16,8,128]{2,1,0:T(8,128)} %bitcast.18), custom_call_target="tpu_custom_call" | custom-call | flops 134217728 | bytes 2097152 | tf_op jit(solution)/shard_map/selfpast/pallas_call | solution.py:246
  60.6 19.1 %all-to-all-done.2.got = s16[8,17,8,128]{3,2,1,0:T(8,128)(2,1)S(1)} async-done(((s16[8,17,8,128]{3,2,1,0:T(8,128)(2,1)}), s16[8,17,8,128]{3,2,1,0:T(8,128)(2,1)S(1)}, u32[]{:S(2)}, u32[]{:S(2)}) %all-to-all-start.2) | async-done | bytes 278560 | tf_op jit(solution)/shard_map/all_to_all | solution.py:245
  79.7 0.0 copy-done
  79.7 2.7 %solve.1 = f32[16,8,128]{2,1,0:T(8,128)} custom-call(s16[8,17,8,128]{3,2,1,0:T(8,128)(2,1)S(1)} %all-to-all-done.2.got, f32[128,128]{1,0:T(8,128)S(1)} %bitcast.12, f32[128,128]{1,0:T(8,128)S(1)} %get-tuple-element.7.base, bf16[15,256,128]{2,1,0:T(8,128)(2,1)S(1)} %get-tuple-element.8.steps), custom_call_target="tpu_custom_call" | custom-call | flops 67108864 | bytes 2097152 | tf_op jit(solution)/shard_map/solve/pallas_call | solution.py:262
Async XLA Ops:
  18.6 4.1 %collective-permute-start = (bf16[8,32,8,128]{3,2,1,0:T(8,128)(2,1)S(1)}, bf16[8,32,8,128]{3,2,1,0:T(8,128)(2,1)S(1)}, u32[]{:S(2)}, u32[]{:S(2)}) collective-permute-start(bf16[8,32,8,128]{3,2,1,0:T(8,128)(2,1)S(1)} %all_to_all.15.past), channel_id=1, source_target_pairs={{0,32},{32,0},{1,33},{33,1},{2,34},{34,2},{3,35},{35,3},{4,36},{36... | collective-permute-start | bytes 1572872 | tf_op jit(solution)/shard_map/ppermute | solution.py:217
  25.2 54.5 %copy-start = (f32[1,1,128,128]{3,2,1,0:T(8,128)S(1)}, f32[1,1,128,128]{3,2,1,0:T(8,128)}, u32[]{:S(2)}) copy-start(f32[1,1,128,128]{3,2,1,0:T(8,128)} %param.14) | copy-start | bytes 196612
  39.9 39.8 %all-to-all-start.2 = ((s16[8,17,8,128]{3,2,1,0:T(8,128)(2,1)}), s16[8,17,8,128]{3,2,1,0:T(8,128)(2,1)S(1)}, u32[]{:S(2)}, u32[]{:S(2)}) async-start(s16[8,17,8,128]{3,2,1,0:T(8,128)(2,1)} %merge.1), calls=%async_computation.2 | async-start | bytes 557056 | tf_op jit(solution)/shard_map/all_to_all | solution.py:245
